TPU v7x, 32 devices: a whole 2x2x4 slice. The times are simulated.
32 devices in a mesh: groups: 2 (over y), row: 4 (over z), col: 2 (over x), sub: 2 (over core).
Axes of the slice: x: 2, y: 2, z: 4, core: 2. Of those that a mesh axis runs over, the one named last changes fastest.
Arguments:
- stream_in: bfloat16 [4096, 5376], P(('groups', 'row'), ('col', 'sub')), parts along dimension 0, may hold values from -6 to 6
- in_gain: float32 [5376], replicated, may hold values from 0.1 to 1.9
- query_weight: bfloat16 [5376, 4096], P('row', ('col', 'sub')), may hold values from -0.078125 to 0.078125
- key_matrix: bfloat16 [5376, 2048], P('row', ('col', 'sub')), may hold values from -0.078125 to 0.078125
- value_matrix: bfloat16 [5376, 2048], P('row', ('col', 'sub')), may hold values from -0.078125 to 0.078125
- query_gain: float32 [128], replicated, may hold values from 0.45 to 10, as said below
- key_norm_gain: float32 [128], replicated, may hold values from 0.45 to 10, as said below
- output_weight: bfloat16 [4096, 5376], P('row', ('col', 'sub')), may hold values from -3 to 3
- post_gain: float32 [5376], P(('col', 'sub')), may hold values from 0.1 to 1.9
Outputs:
- stream_out: bfloat16 [4096, 5376], P(('groups', 'row'), ('col', 'sub')), parts along dimension 0
There are 2 independent parts, one for each index of `groups`. A program takes and returns all parts, laid end to end along the dimension named above; an argument that names none is the same for every part. Nothing has to cross between parts.
Inputs may be any that keep to these rules, and one draw needn't show every extreme that they name: `query_gain`: positive. `key_norm_gain`: positive.
All inputs are finite; a program needn't handle non-finite values.
Results may differ from a plain program's by a relative error of at most 0.014.
The roundings to bfloat16 on the way count: a program that leaves them out, or rounds other values in their place, can miss the bound.
Values may be sent and summed in bfloat16 or wider, within the bound.
A program may use at most 128 MiB of HBM per device.

v0:
```python
import jax
import jax.numpy as jnp
from jax import lax
from jax.sharding import PartitionSpec as P

MODEL_WIDTH = 5376
QUERY_HEAD_COUNT = 32
WINDOW_LENGTH = 1024
EPSILON = 1e-06


def shifted(x, axis, by):
    count = lax.axis_size(axis)
    pairs = [(i, i + by) for i in range(count) if 0 <= i + by < count]
    return lax.ppermute(x, axis, pairs)


def root_mean_scale(values, gain):
    return values * lax.rsqrt(jnp.mean(values * values, axis=-1, keepdims=True) + EPSILON) * gain


def apply_rotary(tensor, token_positions):
    half_dim = tensor.shape[-1] // 2
    inverse = 10000.0 ** (-(jnp.arange(half_dim, dtype=jnp.float32) * 2.0) / tensor.shape[-1])
    angles = token_positions[:, None] * inverse[None, :]
    cosine = jnp.cos(angles)[:, None, :]
    sine_part = jnp.sin(angles)[:, None, :]
    first_half = tensor[..., :half_dim]
    second_half = tensor[..., half_dim:]
    return jnp.concatenate(
        [
            first_half * cosine - second_half * sine_part,
            second_half * cosine + first_half * sine_part,
        ],
        axis=-1,
    )


def on_device(
    stream_in,
    in_gain,
    query_weight,
    key_matrix,
    value_matrix,
    query_gain,
    key_norm_gain,
    output_weight,
    post_gain,
):
    token_rows = lax.all_gather(stream_in, ("col", "sub"), axis=1, tiled=True)
    tokens = token_rows.shape[0]
    normed = root_mean_scale(token_rows.astype(jnp.float32), in_gain).astype(jnp.bfloat16)

    def add_panel(panel_piece):
        return jnp.dot(normed, panel_piece, preferred_element_type=jnp.float32)

    query_proj = add_panel(lax.all_gather(query_weight, "row", axis=0, tiled=True))
    projected_keys = add_panel(lax.all_gather(key_matrix, "row", axis=0, tiled=True))
    projected_values = add_panel(lax.all_gather(value_matrix, "row", axis=0, tiled=True))
    head_size = query_gain.shape[0]
    query_heads = query_weight.shape[1] // head_size
    pair_heads = key_matrix.shape[1] // head_size
    group_count = query_heads // pair_heads
    scale_factor = float(MODEL_WIDTH // QUERY_HEAD_COUNT) ** (-0.5)
    row_index = lax.axis_index("row")
    query_places = row_index * tokens + jnp.arange(tokens, dtype=jnp.int32)
    query_rot = apply_rotary(
        root_mean_scale(query_proj.reshape(tokens, query_heads, head_size), query_gain),
        query_places.astype(jnp.float32),
    ).astype(jnp.bfloat16)
    rotary_keys = apply_rotary(
        root_mean_scale(projected_keys.reshape(tokens, pair_heads, head_size), key_norm_gain),
        query_places.astype(jnp.float32),
    ).astype(jnp.bfloat16)
    keys_flat = rotary_keys.reshape(tokens, pair_heads * head_size)
    values_flat = projected_values.astype(jnp.bfloat16)
    shards_back = min(WINDOW_LENGTH // tokens, lax.axis_size("row") - 1)
    band_length = (shards_back + 1) * tokens
    key_parts = [keys_flat]
    value_parts = [values_flat]
    for offset in range(1, shards_back + 1):
        keys_prior, values_prior = shifted((keys_flat, values_flat), "row", offset)
        key_parts = [keys_prior] + key_parts
        value_parts = [values_prior] + value_parts
    keys_band = jnp.concatenate(key_parts, axis=0)
    values_band = jnp.concatenate(value_parts, axis=0)
    key_places = (row_index - shards_back) * tokens + jnp.arange(band_length, dtype=jnp.int32)
    distance = query_places[:, None] - key_places[None, :]
    visible = (distance >= 0) & (distance < WINDOW_LENGTH) & (key_places[None, :] >= 0)
    grouped = query_rot.reshape(tokens, pair_heads, group_count, head_size)
    scores = (
        jnp.einsum(
            "qhgd,shd->hgqs",
            grouped,
            keys_band.reshape(band_length, pair_heads, head_size),
            preferred_element_type=jnp.float32,
        )
        * scale_factor
    )
    scores = jnp.where(visible, scores, -1e30)
    row_max = jnp.max(scores, axis=-1, keepdims=True)
    exponent = jnp.exp(scores - row_max)
    weights = (exponent / jnp.sum(exponent, axis=-1, keepdims=True)).astype(jnp.bfloat16)
    attended = jnp.einsum(
        "hgqs,shd->qhgd",
        weights,
        values_band.reshape(band_length, pair_heads, head_size),
        preferred_element_type=jnp.float32,
    )
    heads_out = attended.reshape(tokens, query_heads * head_size).astype(jnp.bfloat16)
    head_rows = lax.all_gather(heads_out, ("col", "sub"), axis=1, tiled=True)
    branch = jnp.dot(
        head_rows,
        lax.all_gather(output_weight, "row", axis=0, tiled=True),
        preferred_element_type=jnp.float32,
    )
    squares = lax.psum(jnp.sum(branch * branch, axis=-1), ("col", "sub"))
    scaled = branch * lax.rsqrt(squares[:, None] / MODEL_WIDTH + EPSILON) * post_gain
    return (stream_in.astype(jnp.float32) + scaled).astype(jnp.bfloat16)


def solution(mesh):
    placed = (
        P(("groups", "row"), ("col", "sub")),
        P(),
        P("row", ("col", "sub")),
        P("row", ("col", "sub")),
        P("row", ("col", "sub")),
        P(),
        P(),
        P("row", ("col", "sub")),
        P(("col", "sub")),
    )
    return jax.shard_map(
        on_device,
        mesh=mesh,
        in_specs=placed,
        out_specs=P(("groups", "row"), ("col", "sub")),
        check_vma=False,
    )
```

profile of v0, /device:TPU:0, one launch (start us, length us, event | category | flops | bytes accessed | tf_op | source)
XLA Modules:
  0.0 759.0 jit_solution(18262040499544532429)
XLA Ops:
  11.0 42.5 %all-gather.7.cloned.1.call-done = bf16[512,5376]{0,1:T(8,128)(2,1)} async-done(((bf16[512,1344]{0,1:T(8,128)(2,1)}), bf16[512,5376]{0,1:T(8,128)(2,1)}) %all-gather.7.cloned.1.call-update) | async-done | bytes 5505040 | tf_op jit(solution)/shard_map/all_gather | solution.py:50
  53.5 3.8 fusion.6
  57.3 100.2 %all-gather.11.cloned.1.call-done = bf16[5376,512]{1,0:T(8,128)(2,1)} async-done(((bf16[1344,512]{1,0:T(8,128)(2,1)}), bf16[5376,512]{1,0:T(8,128)(2,1)}) %all-gather.11.cloned.1.call-update) | async-done | bytes 5505040 | tf_op jit(solution)/shard_map/all_gather | solution.py:58
  157.5 7.6 %multiply_reduce_fusion.2 = (f32[512,4]{0,1:T(4,128)S(1)}, f32[512,512]{0,1:T(8,128)S(1)}) fusion(bf16[5376,512]{1,0:T(8,128)(2,1)} %all-gather.11.cloned.1.call-done, bf16[512,5376]{0,1:T(8,128)(2,1)} %all-gather.7.cloned.1.call-done, f32[5376]{0:T(1024)S(1)} %copy-done.6, f32[512]{0:T(512)S(1)} %add_rsqrt_fusion.3), kind=kOutput, calls=%fused_computation.35 | convolution fusion | flops 2830104576 | bytes 12090368 | tf_op jit(solution)/shard_map/dot_general | solution.py:55
  166.8 2.7 collective-permute-start.2
  169.4 2.2 collective-permute-start.3
  171.6 106.4 %all-gather.9.cloned.1.call-done = bf16[5376,512]{1,0:T(8,128)(2,1)} async-done(((bf16[1344,512]{1,0:T(8,128)(2,1)}), bf16[5376,512]{1,0:T(8,128)(2,1)}) %all-gather.9.cloned.1.call-update) | async-done | bytes 5505040 | tf_op jit(solution)/shard_map/all_gather | solution.py:59
  278.1 7.4 convolution_convert_fusion
  285.4 5.1 collective-permute-start
  290.6 16.2 %collective-permute-start.1 = (bf16[512,512]{1,0:T(8,128)(2,1)S(1)}, bf16[512,512]{1,0:T(8,128)(2,1)}, u32[]{:S(2)}, u32[]{:S(2)}) collective-permute-start(bf16[512,512]{1,0:T(8,128)(2,1)S(1)} %convolution_convert_fusion), channel_id=1, source_target_pairs={{0,4},{4,8},{8,12},{1,5},{5,9},{9,13},{2,6},{6,10},{10,14},{3,7},{... | collective-permute-start | bytes 1572872 | tf_op jit(solution)/shard_map/ppermute | solution.py:15
  306.8 1.9 fusion.12
  310.7 18.4 %collective-permute-done.1 = bf16[512,512]{1,0:T(8,128)(2,1)} collective-permute-done((bf16[512,512]{1,0:T(8,128)(2,1)S(1)}, bf16[512,512]{1,0:T(8,128)(2,1)}, u32[]{:S(2)}, u32[]{:S(2)}) %collective-permute-start.1) | collective-permute-done | bytes 524320 | tf_op jit(solution)/shard_map/ppermute | solution.py:15
  329.1 1.3 pad_maximum_fusion
  330.5 1.6 copy.45
  332.1 160.1 %all-gather.13.cloned.1.call-done = bf16[5376,1024]{1,0:T(8,128)(2,1)} async-done(((bf16[1344,1024]{1,0:T(8,128)(2,1)}), bf16[5376,1024]{1,0:T(8,128)(2,1)}) %all-gather.13.cloned.1.call-update) | async-done | bytes 11010064 | tf_op jit(solution)/shard_map/all_gather | solution.py:57
  492.2 11.7 %convolution_bitcast_fusion = f32[64,8,8,128]{3,1,2,0:T(8,128)S(1)} fusion(bf16[5376,1024]{1,0:T(8,128)(2,1)} %all-gather.13.cloned.1.call-done, bf16[512,5376]{0,1:T(8,128)(2,1)} %all-gather.7.cloned.1.call-done, f32[5376]{0:T(1024)S(1)} %copy-done.6, f32[512]{0:T(512)S(1)} %add_rsqrt_fusion.3), kind=kOutput, calls=%fused_computation.25 | convolution fusion | flops 5648154624 | bytes 18635776 | tf_op jit(solution)/shard_map/dot_general | solution.py:55
  508.4 14.3 %fusion.14 = f32[4,1536,512,2]{2,1,3,0:T(8,128)} fusion(bf16[512,4,128]{2,0,1:T(8,128)(2,1)S(1)} %maximum_convert_fusion, bf16[512,4,128]{2,0,1:T(8,128)(2,1)S(1)} %copy-done.2, bf16[512,4,128]{2,0,1:T(8,128)(2,1)S(1)} %copy-done.1, bf16[512,4,2,64]{3,0,2,1:T(8,128)(2,1)S(1)} %bitcast.48, bf16[512,4,2,64]{3,0,2,1:T(8,128)(2,1)S(1)} %bitcast.50), kind=kOutput, calls=%fused_computation.36 | convolution fusion | flops 1617428480 | bytes 27787264 | tf_op jit(solution)/shard_map/qhgd,shd->hgqs/dot_general | solution.py:92
  522.7 10.5 %fusion.30 = f32[4,2,512]{2,1,0:T(2,128)S(1)} fusion(pred[512,1536]{0,1:T(8,128)(4,1)} %fusion.12, bf16[512,4,128]{2,0,1:T(8,128)(2,1)S(1)} %maximum_convert_fusion, bf16[512,4,128]{2,0,1:T(8,128)(2,1)} %copy.35, bf16[512,4,128]{2,0,1:T(8,128)(2,1)S(1)} %copy-done.1, bf16[512,4,2,64]{3,0,2,1:T(8,128)(2,1)S(1)} %bitcast.49, ...), kind=kOutput, calls=%fused_computation.56 | convolution fusion | flops 1642595840 | bytes 3424256 | tf_op jit(solution)/shard_map/sub | solution.py:102
  533.2 15.3 %fusion.13 = bf16[4,128,2,512]{3,1,2,0:T(8,128)(2,1)} fusion(bf16[1536,4,128,1]{0,2,3,1:T(8,128)(2,1)} %bitcast.52, f32[4,2,512]{2,1,0:T(2,128)S(1)} %fusion.30, f32[4,1536,512,2]{2,1,3,0:T(8,128)} %fusion.14, pred[512,1536]{0,1:T(8,128)(4,1)} %fusion.12), kind=kOutput, calls=%fused_computation.28 | convolution fusion | flops 1642599936 | bytes 28590080 | tf_op jit(solution)/shard_map/hgqs,shd->qhgd/dot_general | solution.py:104
  548.5 149.4 %all-gather.17.cloned.1.call-done = bf16[4096,1344]{0,1:T(8,128)(2,1)} async-done(((bf16[1024,1344]{0,1:T(8,128)(2,1)}), bf16[4096,1344]{0,1:T(8,128)(2,1)}) %all-gather.17.cloned.1.call-update) | async-done | bytes 11010064 | tf_op jit(solution)/shard_map/all_gather | solution.py:114
  697.9 34.1 %all-gather.15.cloned.1.call-done = bf16[512,4096]{0,1:T(8,128)(2,1)} async-done(((bf16[512,1024]{0,1:T(8,128)(2,1)}), bf16[512,4096]{0,1:T(8,128)(2,1)}) %all-gather.15.cloned.1.call-update) | async-done | bytes 4194320 | tf_op jit(solution)/shard_map/all_gather | solution.py:111
  732.0 10.9 %multiply_reduce_fusion = (f32[512]{0:T(512)S(1)}, f32[512,1344]{0,1:T(8,128)}) fusion(bf16[4096,1344]{0,1:T(8,128)(2,1)} %all-gather.17.cloned.1.call-done, bf16[512,4096]{0,1:T(8,128)(2,1)} %all-gather.15.cloned.1.call-done), kind=kOutput, calls=%fused_computation.20 | convolution fusion | flops 5638520320 | bytes 17958912 | tf_op jit(solution)/shard_map/dot_general | solution.py:112
  742.9 5.9 psum.7
  748.8 3.3 add_convert_fusion
  (54 shorter events, 12.5 us)
Async XLA Ops:
  6.5 47.0 %all-gather.7.cloned.1.call-start = ((), (), s32[]{:S(2)}) async-start(), calls=%async_computation | async-start | bytes 6881280 | tf_op jit(solution)/shard_map/all_gather | solution.py:50
  7.3 150.2 %all-gather.11.cloned.1.call-start = ((), (), s32[]{:S(2)}) async-start(), calls=%async_computation.2 | async-start | bytes 6881280 | tf_op jit(solution)/shard_map/all_gather | solution.py:58
  8.0 270.0 %all-gather.9.cloned.1.call-start = ((), (), s32[]{:S(2)}) async-start(), calls=%async_computation.1 | async-start | bytes 6881280 | tf_op jit(solution)/shard_map/all_gather | solution.py:59
  8.7 483.4 %all-gather.13.cloned.1.call-start = ((), (), s32[]{:S(2)}) async-start(), calls=%async_computation.3 | async-start | bytes 13762560 | tf_op jit(solution)/shard_map/all_gather | solution.py:57
  9.3 688.6 %all-gather.17.cloned.1.call-start = ((), (), s32[]{:S(2)}) async-start(), calls=%async_computation.5 | async-start | bytes 13762560 | tf_op jit(solution)/shard_map/all_gather | solution.py:114
  9.9 147.6 %copy-start.6 = (f32[5376]{0:T(1024)S(1)}, f32[5376]{0:T(1024)}, u32[]{:S(2)}) copy-start(f32[5376]{0:T(1024)} %param.10) | copy-start | bytes 64516
  9.9 722.1 %all-gather.15.cloned.1.call-start = ((), (), s32[]{:S(2)}) async-start(), calls=%async_computation.4 | async-start | bytes 5242880 | tf_op jit(solution)/shard_map/all_gather | solution.py:111
  57.3 108.2 %copy-start.4 = (f32[128]{0:T(128)S(1)}, f32[128]{0:T(128)}, u32[]{:S(2)}) copy-start(f32[128]{0:T(128)} %param.15) | copy-start | bytes 1540
  166.8 141.9 %collective-permute-start.2 = (bf16[512,512]{0,1:T(8,128)(2,1)S(1)}, bf16[512,512]{0,1:T(8,128)(2,1)S(1)}, u32[]{:S(2)}, u32[]{:S(2)}) collective-permute-start(bf16[512,512]{0,1:T(8,128)(2,1)S(1)} %bitcast.55), channel_id=1, source_target_pairs={{0,8},{4,12},{1,9},{5,13},{2,10},{6,14},{3,11},{7,15},{16,24},{20,... | collective-permute-start | bytes 1572872 | tf_op jit(solution)/shard_map/ppermute | solution.py:15
  169.4 140.3 %collective-permute-start.3 = (bf16[512,512]{0,1:T(8,128)(2,1)S(1)}, bf16[512,512]{0,1:T(8,128)(2,1)S(1)}, u32[]{:S(2)}, u32[]{:S(2)}) collective-permute-start(bf16[512,512]{0,1:T(8,128)(2,1)S(1)} %bitcast.56), channel_id=1, source_target_pairs={{0,4},{4,8},{8,12},{1,5},{5,9},{9,13},{2,6},{6,10},{10,14},{3,7},{... | collective-permute-start | bytes 1572872 | tf_op jit(solution)/shard_map/ppermute | solution.py:15
  285.4 25.3 %collective-permute-start = (bf16[512,512]{1,0:T(8,128)(2,1)S(1)}, bf16[512,512]{1,0:T(8,128)(2,1)}, u32[]{:S(2)}, u32[]{:S(2)}) collective-permute-start(bf16[512,512]{1,0:T(8,128)(2,1)S(1)} %convolution_convert_fusion), channel_id=1, source_target_pairs={{0,8},{4,12},{1,9},{5,13},{2,10},{6,14},{3,11},{7,15},{16,24},{20,... | collective-permute-start | bytes 1572872 | tf_op jit(solution)/shard_map/ppermute | solution.py:15
  290.6 38.6 %collective-permute-start.1 = (bf16[512,512]{1,0:T(8,128)(2,1)S(1)}, bf16[512,512]{1,0:T(8,128)(2,1)}, u32[]{:S(2)}, u32[]{:S(2)}) collective-permute-start(bf16[512,512]{1,0:T(8,128)(2,1)S(1)} %convolution_convert_fusion), channel_id=1, source_target_pairs={{0,4},{4,8},{8,12},{1,5},{5,9},{9,13},{2,6},{6,10},{10,14},{3,7},{... | collective-permute-start | bytes 1572872 | tf_op jit(solution)/shard_map/ppermute | solution.py:15
  503.9 1.4 copy-start.5
  507.2 1.0 copy-start.1
  507.2 1.2 copy-start.2
  548.5 200.3 %copy-start = (bf16[512,1344]{0,1:T(8,128)(2,1)S(1)}, bf16[512,1344]{0,1:T(8,128)(2,1)}, u32[]{:S(2)}) copy-start(bf16[512,1344]{0,1:T(8,128)(2,1)} %param.9) | copy-start | bytes 4128772
  548.5 200.3 %copy-start.3 = (f32[1344]{0:T(1024)S(1)}, f32[1344]{0:T(1024)}, u32[]{:S(2)}) copy-start(f32[1344]{0:T(1024)} %param.17) | copy-start | bytes 16132
Sparse Core Ops, SparseCore 0:
  8.9 44.6 all-gather.6
  55.1 102.3 all-gather.10
  159.1 118.9 all-gather.8
  279.5 212.6 all-gather.12
  493.6 204.2 all-gather.16
  699.3 32.6 all-gather.14
where the time goes:
time: 759 us
  waiting for transfers between devices  614 us (81%)
  matrix products  77.7 us (10%)
  starting transfers between devices  26.3 us (3%)
  other arithmetic  15 us (2%)
  between operations  13.7 us (2%)
    all_gather x1, waiting for transfers between devices, on_device(): lax.all_gather(query_weight, 'row', axis=0, tiled=True)  160 us
    all_gather x1, waiting for transfers between devices, on_device(): lax.all_gather(output_weight, 'row', axis=0, tiled=True)  149 us
    all_gather x1, waiting for transfers between devices, on_device(): lax.all_gather(value_matrix, 'row', axis=0, tiled=True)  106 us
    all_gather x1, waiting for transfers between devices, on_device(): lax.all_gather(key_matrix, 'row', axis=0, tiled=True)  100 us
    all_gather x1, waiting for transfers between devices, on_device(): token_rows = lax.all_gather(stream_in, ('col', 'sub'), axis=1, tiled=True)  42.5 us
    all_gather x1, waiting for transfers between devices, on_device(): head_rows = lax.all_gather(heads_out, ('col', 'sub'), axis=1, tiled=True)  34.1 us
    dot_general x3, matrix products, add_panel(): return jnp.dot(normed, panel_piece, preferred_element_type=jnp.float32)  26.7 us
    ppermute x4, starting transfers between devices, shifted(): return lax.ppermute(x, axis, pairs)  26.1 us
  transfers between devices with their start and end apart: 10, of which 7 were waited for; matrix products, arithmetic and copies ran while one was open for 11% of the time, Pallas kernels for 0%

commit v1 on v0

--- a/solution.py
+++ b/solution.py
@@ -2,11 +2,29 @@
 import jax.numpy as jnp
 from jax import lax
 from jax.sharding import PartitionSpec as P
+from jax.lax import axis_index, axis_size, ppermute
 
 MODEL_WIDTH = 5376
 QUERY_HEAD_COUNT = 32
 WINDOW_LENGTH = 1024
 EPSILON = 1e-06
+
+
+def create_the_sector(arr_in, axis_tag):
+    tile_out = axis_index(axis_tag)
+    now = axis_size(axis_tag)
+    bank = []
+    block_next, later, odd = (now, tile_out, arr_in.shape[0])
+    for w in range(block_next):
+        bank.append((w, (w + 1) % block_next))
+    everything = jnp.zeros((*arr_in.shape[:0], block_next * odd, *arr_in.shape[1:]), arr_in.dtype)
+    carry_in = arr_in
+    for dev_i in range(block_next):
+        a_now = (later - dev_i) % block_next
+        everything = lax.dynamic_update_slice_in_dim(everything, carry_in, a_now * odd, axis=0)
+        if dev_i < block_next - 1:
+            carry_in = ppermute(carry_in, axis_tag, bank)
+    return everything
 
 
 def shifted(x, axis, by):
@@ -110,9 +128,7 @@
     heads_out = attended.reshape(tokens, query_heads * head_size).astype(jnp.bfloat16)
     head_rows = lax.all_gather(heads_out, ("col", "sub"), axis=1, tiled=True)
     branch = jnp.dot(
-        head_rows,
-        lax.all_gather(output_weight, "row", axis=0, tiled=True),
-        preferred_element_type=jnp.float32,
+        head_rows, create_the_sector(output_weight, "row"), preferred_element_type=jnp.float32
     )
     squares = lax.psum(jnp.sum(branch * branch, axis=-1), ("col", "sub"))
     scaled = branch * lax.rsqrt(squares[:, None] / MODEL_WIDTH + EPSILON) * post_gain

time: 759 us -> 729 us (0.960); the launches traced: 759 us -> 720 us
  waiting for transfers between devices: 614 us -> 545 us
  local copies, waits for them, and re-layouts: 6.05 us -> 24.4 us
  starting transfers between devices: 26.3 us -> 42 us
    all_gather x1 -> x0, waiting for transfers between devices: 149 us -> none  [on_device(): lax.all_gather(output_weight, 'row', axis=0, tiled=True)]
    ppermute x0 -> x3, waiting for transfers between devices: none -> 111 us  [create_the_sector(): carry_in = ppermute(carry_in, axis_tag, bank)]
    all_gather x1, waiting for transfers between devices: 34.1 us -> 0.01 us  [on_device(): head_rows = lax.all_gather(heads_out, ('col', 'sub'), axis=1, tiled=True)]
    ppermute x0 -> x3, starting transfers between devices: none -> 14.2 us  [create_the_sector(): carry_in = ppermute(carry_in, axis_tag, bank)]
    dynamic_update_slice x0 -> x4, local copies, waits for them, and re-layouts: none -> 12.8 us  [create_the_sector(): lax.dynamic_update_slice_in_dim(everything, carry_in, a_now * odd, axis=0)]
  transfers between devices with their start and end apart: 10 -> 12, of which waited for: 7 -> 7; matrix products, arithmetic and copies ran while one was open for 11% -> 14% of each run, Pallas kernels for 0% -> 0%
where the time goes in v1:
time: 729 us; the launch traced here: 720 us
  waiting for transfers between devices  545 us (75%)
  matrix products  75.2 us (10%)
  starting transfers between devices  42 us (6%)
  local copies, waits for them, and re-layouts  24.4 us (3%)
  other arithmetic  15 us (2%)
  between operations  13.6 us (2%)
    all_gather x1, waiting for transfers between devices, on_device(): lax.all_gather(query_weight, 'row', axis=0, tiled=True)  160 us
    ppermute x3, waiting for transfers between devices, create_the_sector(): carry_in = ppermute(carry_in, axis_tag, bank)  111 us
    all_gather x1, waiting for transfers between devices, on_device(): lax.all_gather(key_matrix, 'row', axis=0, tiled=True)  106 us
    all_gather x1, waiting for transfers between devices, on_device(): lax.all_gather(value_matrix, 'row', axis=0, tiled=True)  106 us
    all_gather x1, waiting for transfers between devices, on_device(): token_rows = lax.all_gather(stream_in, ('col', 'sub'), axis=1, tiled=True)  40 us
    ppermute x4, starting transfers between devices, shifted(): return lax.ppermute(x, axis, pairs)  27.7 us
    dot_general x3, matrix products, add_panel(): return jnp.dot(normed, panel_piece, preferred_element_type=jnp.float32)  26.7 us
    ppermute x4, waiting for transfers between devices, shifted(): return lax.ppermute(x, axis, pairs)  17.9 us
  transfers between devices with their start and end apart: 12, of which 7 were waited for; matrix products, arithmetic and copies ran while one was open for 14% of the time, Pallas kernels for 0%

profile of v1, /device:TPU:0, one launch (start us, length us, event | category | flops | bytes accessed | tf_op | source)
XLA Modules:
  0.0 720.4 jit_solution(6939861807186631846)
XLA Ops:
  13.5 40.0 %all-gather.6.cloned.1.call-done = bf16[512,5376]{0,1:T(8,128)(2,1)} async-done(((bf16[512,1344]{0,1:T(8,128)(2,1)}), bf16[512,5376]{0,1:T(8,128)(2,1)}) %all-gather.6.cloned.1.call-update) | async-done | bytes 5505040 | tf_op jit(solution)/shard_map/all_gather | solution.py:68
  53.5 3.8 fusion.6
  57.3 106.4 %all-gather.10.cloned.1.call-done = bf16[5376,512]{1,0:T(8,128)(2,1)} async-done(((bf16[1344,512]{1,0:T(8,128)(2,1)}), bf16[5376,512]{1,0:T(8,128)(2,1)}) %all-gather.10.cloned.1.call-update) | async-done | bytes 5505040 | tf_op jit(solution)/shard_map/all_gather | solution.py:76
  163.7 7.6 %multiply_reduce_fusion.2 = (f32[512,4]{0,1:T(4,128)S(1)}, f32[512,512]{0,1:T(8,128)S(1)}) fusion(bf16[5376,512]{1,0:T(8,128)(2,1)} %all-gather.10.cloned.1.call-done, bf16[512,5376]{0,1:T(8,128)(2,1)} %all-gather.6.cloned.1.call-done, f32[5376]{0:T(1024)S(1)} %copy-done.6, f32[512]{0:T(512)S(1)} %add_rsqrt_fusion.3), kind=kOutput, calls=%fused_computation.35 | convolution fusion | flops 2830104576 | bytes 12090368 | tf_op jit(solution)/shard_map/dot_general | solution.py:73
  175.5 3.4 collective-permute-start.3
  178.9 106.2 %all-gather.8.cloned.1.call-done = bf16[5376,512]{1,0:T(8,128)(2,1)} async-done(((bf16[1344,512]{1,0:T(8,128)(2,1)}), bf16[5376,512]{1,0:T(8,128)(2,1)}) %all-gather.8.cloned.1.call-update) | async-done | bytes 5505040 | tf_op jit(solution)/shard_map/all_gather | solution.py:77
  285.1 7.4 %convolution_convert_fusion = bf16[512,512]{1,0:T(8,128)(2,1)S(1)} fusion(bf16[5376,512]{1,0:T(8,128)(2,1)} %all-gather.8.cloned.1.call-done, bf16[512,5376]{0,1:T(8,128)(2,1)} %all-gather.6.cloned.1.call-done, f32[5376]{0:T(1024)S(1)} %copy-done.6, f32[512]{0:T(512)S(1)} %add_rsqrt_fusion.3), kind=kOutput, calls=%fused_computation.29 | convolution fusion | flops 2829844480 | bytes 11557888 | tf_op jit(solution)/shard_map/dot_general | solution.py:73
  292.5 5.1 collective-permute-start
  297.6 16.6 %collective-permute-start.1 = (bf16[512,512]{1,0:T(8,128)(2,1)S(1)}, bf16[512,512]{1,0:T(8,128)(2,1)}, u32[]{:S(2)}, u32[]{:S(2)}) collective-permute-start(bf16[512,512]{1,0:T(8,128)(2,1)S(1)} %convolution_convert_fusion), channel_id=1, source_target_pairs={{0,4},{4,8},{8,12},{1,5},{5,9},{9,13},{2,6},{6,10},{10,14},{3,7},{... | collective-permute-start | bytes 1572872 | tf_op jit(solution)/shard_map/ppermute | solution.py:33
  318.3 17.9 %collective-permute-done.1 = bf16[512,512]{1,0:T(8,128)(2,1)} collective-permute-done((bf16[512,512]{1,0:T(8,128)(2,1)S(1)}, bf16[512,512]{1,0:T(8,128)(2,1)}, u32[]{:S(2)}, u32[]{:S(2)}) %collective-permute-start.1) | collective-permute-done | bytes 524320 | tf_op jit(solution)/shard_map/ppermute | solution.py:33
  339.1 160.1 %all-gather.12.cloned.1.call-done = bf16[5376,1024]{1,0:T(8,128)(2,1)} async-done(((bf16[1344,1024]{1,0:T(8,128)(2,1)}), bf16[5376,1024]{1,0:T(8,128)(2,1)}) %all-gather.12.cloned.1.call-update) | async-done | bytes 11010064 | tf_op jit(solution)/shard_map/all_gather | solution.py:75
  499.2 11.7 %convolution_bitcast_fusion = f32[64,8,8,128]{3,1,2,0:T(8,128)S(1)} fusion(bf16[5376,1024]{1,0:T(8,128)(2,1)} %all-gather.12.cloned.1.call-done, bf16[512,5376]{0,1:T(8,128)(2,1)} %all-gather.6.cloned.1.call-done, f32[5376]{0:T(1024)S(1)} %copy-done.6, f32[512]{0:T(512)S(1)} %add_rsqrt_fusion.3), kind=kOutput, calls=%fused_computation.25 | convolution fusion | flops 5648154624 | bytes 18635776 | tf_op jit(solution)/shard_map/dot_general | solution.py:73
  515.4 11.8 %fusion.14 = f32[4,1536,512,2]{2,1,3,0:T(8,128)} fusion(bf16[512,4,128]{2,0,1:T(8,128)(2,1)S(1)} %maximum_convert_fusion, bf16[512,4,128]{2,0,1:T(8,128)(2,1)S(1)} %copy-done.2, bf16[512,4,128]{2,0,1:T(8,128)(2,1)S(1)} %copy-done.1, bf16[512,4,2,64]{3,0,2,1:T(8,128)(2,1)S(1)} %bitcast.48, bf16[512,4,2,64]{3,0,2,1:T(8,128)(2,1)S(1)} %bitcast.50), kind=kOutput, calls=%fused_computation.36 | convolution fusion | flops 1617428480 | bytes 27787264 | tf_op jit(solution)/shard_map/qhgd,shd->hgqs/dot_general | solution.py:110
  527.2 10.5 %fusion.30 = f32[4,2,512]{2,1,0:T(2,128)S(1)} fusion(pred[512,1536]{0,1:T(8,128)(4,1)} %fusion.12, bf16[512,4,128]{2,0,1:T(8,128)(2,1)S(1)} %maximum_convert_fusion, bf16[512,4,128]{2,0,1:T(8,128)(2,1)} %copy.35, bf16[512,4,128]{2,0,1:T(8,128)(2,1)S(1)} %copy-done.1, bf16[512,4,2,64]{3,0,2,1:T(8,128)(2,1)S(1)} %bitcast.49, ...), kind=kOutput, calls=%fused_computation.60 | convolution fusion | flops 1642595840 | bytes 3424256 | tf_op jit(solution)/shard_map/sub | solution.py:120
  537.7 15.2 %fusion.13 = bf16[4,128,2,512]{3,1,2,0:T(8,128)(2,1)} fusion(bf16[1536,4,128,1]{0,2,3,1:T(8,128)(2,1)} %bitcast.52, f32[4,2,512]{2,1,0:T(2,128)S(1)} %fusion.30, f32[4,1536,512,2]{2,1,3,0:T(8,128)} %fusion.14, pred[512,1536]{0,1:T(8,128)(4,1)} %fusion.12), kind=kOutput, calls=%fused_computation.28 | convolution fusion | flops 1642599936 | bytes 28590080 | tf_op jit(solution)/shard_map/hgqs,shd->qhgd/dot_general | solution.py:122
  553.0 11.1 %collective-permute-start.5 = (bf16[1024,1344]{0,1:T(8,128)(2,1)}, bf16[1024,1344]{0,1:T(8,128)(2,1)S(1)}, u32[]{:S(2)}, u32[]{:S(2)}) collective-permute-start(bf16[1024,1344]{0,1:T(8,128)(2,1)} %collective-permute-done.4), channel_id=1, source_target_pairs={{0,4},{4,8},{8,12},{12,0},{1,5},{5,9},{9,13},{13,1},{2,6},{6,10},{... | collective-permute-start | bytes 8257544 | tf_op jit(solution)/shard_map/ppermute | solution.py:26
  564.0 63.1 %collective-permute-done.5 = bf16[1024,1344]{0,1:T(8,128)(2,1)S(1)} collective-permute-done((bf16[1024,1344]{0,1:T(8,128)(2,1)}, bf16[1024,1344]{0,1:T(8,128)(2,1)S(1)}, u32[]{:S(2)}, u32[]{:S(2)}) %collective-permute-start.5) | collective-permute-done | bytes 2752544 | tf_op jit(solution)/shard_map/ppermute | solution.py:26
  627.1 5.6 broadcast_in_dim.10
  632.7 3.6 constant_dynamic-update-slice_fusion.3
  636.3 3.6 constant_dynamic-update-slice_fusion.2
  641.8 48.2 %collective-permute-done.6 = bf16[1024,1344]{0,1:T(8,128)(2,1)} collective-permute-done((bf16[1024,1344]{0,1:T(8,128)(2,1)S(1)}, bf16[1024,1344]{0,1:T(8,128)(2,1)}, u32[]{:S(2)}, u32[]{:S(2)}) %collective-permute-start.6) | collective-permute-done | bytes 2752544 | tf_op jit(solution)/shard_map/ppermute | solution.py:26
  690.0 3.6 constant_dynamic-update-slice_fusion
  693.7 11.0 %multiply_reduce_fusion = (f32[512]{0:T(512)S(1)}, f32[512,1344]{0,1:T(8,128)}) fusion(bf16[4096,1344]{0,1:T(8,128)(2,1)} %constant_dynamic-update-slice_fusion, bf16[512,4096]{0,1:T(8,128)(2,1)} %all-gather.14.cloned.1.call-done), kind=kOutput, calls=%fused_computation.20 | convolution fusion | flops 5638520320 | bytes 17958912 | tf_op jit(solution)/shard_map/dot_general | solution.py:130
  704.7 5.6 psum.7
  (62 shorter events, 27.6 us)
Async XLA Ops:
  6.5 47.0 %all-gather.6.cloned.1.call-start = ((), (), s32[]{:S(2)}) async-start(), calls=%async_computation | async-start | bytes 6881280 | tf_op jit(solution)/shard_map/all_gather | solution.py:68
  7.3 156.4 %all-gather.10.cloned.1.call-start = ((), (), s32[]{:S(2)}) async-start(), calls=%async_computation.2 | async-start | bytes 6881280 | tf_op jit(solution)/shard_map/all_gather | solution.py:76
  8.0 277.1 %all-gather.8.cloned.1.call-start = ((), (), s32[]{:S(2)}) async-start(), calls=%async_computation.1 | async-start | bytes 6881280 | tf_op jit(solution)/shard_map/all_gather | solution.py:77
  8.7 490.5 %all-gather.12.cloned.1.call-start = ((), (), s32[]{:S(2)}) async-start(), calls=%async_computation.3 | async-start | bytes 13762560 | tf_op jit(solution)/shard_map/all_gather | solution.py:75
  9.3 154.4 %copy-start.6 = (f32[5376]{0:T(1024)S(1)}, f32[5376]{0:T(1024)}, u32[]{:S(2)}) copy-start(f32[5376]{0:T(1024)} %param.10) | copy-start | bytes 64516
  9.3 684.3 %all-gather.14.cloned.1.call-start = ((), (), s32[]{:S(2)}) async-start(), calls=%async_computation.4 | async-start | bytes 5242880 | tf_op jit(solution)/shard_map/all_gather | solution.py:129
  9.4 543.6 %collective-permute-start.4 = (bf16[1024,1344]{0,1:T(8,128)(2,1)}, bf16[1024,1344]{0,1:T(8,128)(2,1)}, u32[]{:S(2)}, u32[]{:S(2)}) collective-permute-start(bf16[1024,1344]{0,1:T(8,128)(2,1)} %param.16), channel_id=1, source_target_pairs={{0,4},{4,8},{8,12},{12,0},{1,5},{5,9},{9,13},{13,1},{2,6},{6,10},{... | collective-permute-start | bytes 8257544 | tf_op jit(solution)/shard_map/ppermute | solution.py:26
  57.3 114.3 %copy-start.4 = (f32[128]{0:T(128)S(1)}, f32[128]{0:T(128)}, u32[]{:S(2)}) copy-start(f32[128]{0:T(128)} %param.15) | copy-start | bytes 1540
  173.0 143.3 %collective-permute-start.2 = (bf16[512,512]{0,1:T(8,128)(2,1)S(1)}, bf16[512,512]{0,1:T(8,128)(2,1)S(1)}, u32[]{:S(2)}, u32[]{:S(2)}) collective-permute-start(bf16[512,512]{0,1:T(8,128)(2,1)S(1)} %bitcast.55), channel_id=1, source_target_pairs={{0,8},{4,12},{1,9},{5,13},{2,10},{6,14},{3,11},{7,15},{16,24},{20,... | collective-permute-start | bytes 1572872 | tf_op jit(solution)/shard_map/ppermute | solution.py:33
  175.5 141.7 %collective-permute-start.3 = (bf16[512,512]{0,1:T(8,128)(2,1)S(1)}, bf16[512,512]{0,1:T(8,128)(2,1)S(1)}, u32[]{:S(2)}, u32[]{:S(2)}) collective-permute-start(bf16[512,512]{0,1:T(8,128)(2,1)S(1)} %bitcast.56), channel_id=1, source_target_pairs={{0,4},{4,8},{8,12},{1,5},{5,9},{9,13},{2,6},{6,10},{10,14},{3,7},{... | collective-permute-start | bytes 1572872 | tf_op jit(solution)/shard_map/ppermute | solution.py:33
  292.5 25.8 %collective-permute-start = (bf16[512,512]{1,0:T(8,128)(2,1)S(1)}, bf16[512,512]{1,0:T(8,128)(2,1)}, u32[]{:S(2)}, u32[]{:S(2)}) collective-permute-start(bf16[512,512]{1,0:T(8,128)(2,1)S(1)} %convolution_convert_fusion), channel_id=1, source_target_pairs={{0,8},{4,12},{1,9},{5,13},{2,10},{6,14},{3,11},{7,15},{16,24},{20,... | collective-permute-start | bytes 1572872 | tf_op jit(solution)/shard_map/ppermute | solution.py:33
  297.6 38.6 %collective-permute-start.1 = (bf16[512,512]{1,0:T(8,128)(2,1)S(1)}, bf16[512,512]{1,0:T(8,128)(2,1)}, u32[]{:S(2)}, u32[]{:S(2)}) collective-permute-start(bf16[512,512]{1,0:T(8,128)(2,1)S(1)} %convolution_convert_fusion), channel_id=1, source_target_pairs={{0,4},{4,8},{8,12},{1,5},{5,9},{9,13},{2,6},{6,10},{10,14},{3,7},{... | collective-permute-start | bytes 1572872 | tf_op jit(solution)/shard_map/ppermute | solution.py:33
  510.9 1.4 copy-start.5
  514.2 1.0 copy-start.1
  514.2 1.2 copy-start.2
  553.0 74.1 %collective-permute-start.5 = (bf16[1024,1344]{0,1:T(8,128)(2,1)}, bf16[1024,1344]{0,1:T(8,128)(2,1)S(1)}, u32[]{:S(2)}, u32[]{:S(2)}) collective-permute-start(bf16[1024,1344]{0,1:T(8,128)(2,1)} %collective-permute-done.4), channel_id=1, source_target_pairs={{0,4},{4,8},{8,12},{12,0},{1,5},{5,9},{9,13},{13,1},{2,6},{6,10},{... | collective-permute-start | bytes 8257544 | tf_op jit(solution)/shard_map/ppermute | solution.py:26
  627.1 62.9 %collective-permute-start.6 = (bf16[1024,1344]{0,1:T(8,128)(2,1)S(1)}, bf16[1024,1344]{0,1:T(8,128)(2,1)}, u32[]{:S(2)}, u32[]{:S(2)}) collective-permute-start(bf16[1024,1344]{0,1:T(8,128)(2,1)S(1)} %collective-permute-done.5), channel_id=1, source_target_pairs={{0,4},{4,8},{8,12},{12,0},{1,5},{5,9},{9,13},{13,1},{2,6},{6,10},{... | collective-permute-start | bytes 8257544 | tf_op jit(solution)/shard_map/ppermute | solution.py:26
  693.6 16.7 %copy-start = (bf16[512,1344]{0,1:T(8,128)(2,1)S(1)}, bf16[512,1344]{0,1:T(8,128)(2,1)}, u32[]{:S(2)}) copy-start(bf16[512,1344]{0,1:T(8,128)(2,1)} %param.9) | copy-start | bytes 4128772
  693.6 16.7 %copy-start.3 = (f32[1344]{0:T(1024)S(1)}, f32[1344]{0:T(1024)}, u32[]{:S(2)}) copy-start(f32[1344]{0:T(1024)} %param.17) | copy-start | bytes 16132
Sparse Core Ops, SparseCore 0:
  8.9 44.6 all-gather.5
  55.1 108.5 all-gather.9
  165.3 119.7 all-gather.7
  286.5 212.6 all-gather.11
  553.1 46.2 all-gather.13
